TPU v7x, 256 devices: a whole 4x4x8 slice. The times are simulated.
256 devices in a mesh: rows: 16 (over y, z_hi, core), feat: 16 (over z_lo, x).
Axes of the slice: x: 4, y: 4, z: 8 (z_hi: 2, z_lo: 4; z = z_hi * 4 + z_lo), core: 2. Of those that a mesh axis runs over, the one named last changes fastest.
Arguments:
- samples: float32 [24576, 8192], P('rows', 'feat'), may hold values from -6 to 6
- whitening: float32 [8192, 1024], P('feat', 'rows'), may hold values from -0.09375 to 0.09375
- components: float32 [1024, 1024], P('rows', 'feat'), may hold values from -0.25 to 0.25
Outputs:
- moment: float32 [1024, 1024], P('rows', 'feat')
All inputs are finite; a program needn't handle non-finite values.
Results may differ from a plain program's by a relative error of at most 0.00017.
Values sent between devices are 32-bit elements; how exact they have to be, the bound alone decides.
A program may use at most 64 MiB of HBM per device.

v0:
```python
import jax
import jax.numpy as jnp
from jax import lax
from jax.sharding import PartitionSpec as P


def from_everyone(value, axis):
    copies = jnp.broadcast_to(value, (lax.axis_size(axis), *value.shape))
    return lax.all_to_all(copies, axis, split_axis=0, concat_axis=0, tiled=True)


def laid_out(tiles, dim):
    shape = list(tiles.shape[1:])
    shape[dim] *= tiles.shape[0]
    return jnp.moveaxis(tiles, 0, dim).reshape(shape)


def collect(value, axis, dim):
    tiles = from_everyone(value, axis)
    return laid_out(tiles, dim)


def in_blocks(value, dim, peers):
    shape = value.shape
    tiles = value.reshape(*shape[:dim], peers, shape[dim] // peers, *shape[dim + 1 :])
    return jnp.moveaxis(tiles, dim, 0)


def summed_on_arrival(value, axis, dim):
    peers = lax.axis_size(axis)
    tiles = lax.all_to_all(in_blocks(value, dim, peers), axis, 0, 0, tiled=True)
    return jnp.sum(tiles, axis=0)


def on_device(samples, whitening, components):
    partial_y = jnp.dot(
        samples,
        collect(whitening, "rows", 1),
        precision=lax.Precision.HIGHEST,
        preferred_element_type=jnp.float32,
    )
    whitened = lax.psum(partial_y, "feat")
    local_rows = whitened.shape[0]
    columns = whitened
    projected = jnp.dot(
        columns,
        collect(components, "rows", 0),
        precision=lax.Precision.HIGHEST,
        preferred_element_type=jnp.float32,
    )
    squared = projected * projected
    scale_inv = 1.0 / jnp.sqrt(jnp.float32(local_rows * lax.axis_size("rows")))
    columns = whitened
    product = lax.dot_general(
        columns,
        squared,
        (((0,), (0,)), ((), ())),
        precision=lax.Precision.HIGHEST,
        preferred_element_type=jnp.float32,
    )
    return summed_on_arrival(product * scale_inv, "rows", 0)


def solution(mesh):
    placed = (P("rows", "feat"), P("feat", "rows"), P("rows", "feat"))
    return jax.shard_map(
        on_device, mesh=mesh, in_specs=placed, out_specs=P("rows", "feat"), check_vma=False
    )
```

profile of v0, /device:TPU:1, one launch (start us, length us, event | category | flops | bytes accessed | tf_op | source)
XLA Modules:
  0.0 322.7 jit_solution(18132606705993271386)
XLA Ops:
  6.5 0.0 copy-start
  6.5 0.0 all-reduce.2.cloned.1.call-start
  6.5 1.3 broadcast_in_dim.6
  7.9 49.0 %all_to_all.15 = f32[16,512,64]{1,2,0:T(8,128)S(1)} all-to-all(f32[16,512,64]{1,2,0:T(8,128)S(1)} %broadcast_in_dim.6), channel_id=1, replica_groups=mesh['rows'=16,'feat'=16] {'rows'}, dimensions={0} | all-to-all | bytes 4194304 | tf_op jit(solution)/shard_map/all_to_all | solution.py:9
  56.9 0.0 copy-done
  56.9 12.1 %fusion = f32[1536,1024]{1,0:T(8,128)} fusion(f32[1536,512]{1,0:T(8,128)S(1)} %copy-done, f32[512,1024]{0,1:T(8,128)S(1)} %bitcast.17), kind=kOutput, calls=%fused_computation.4 | convolution fusion | flops 9663676416 | bytes 11534336 | tf_op jit(solution)/shard_map/dot_general | solution.py:36
  68.9 0.0 copy-start.2
  68.9 0.0 all-reduce.2.cloned.1.call-update
  69.0 0.7 copy-done.2
  69.7 0.9 broadcast_in_dim.7
  70.6 1.4 reshape.12
  71.9 34.4 %all_to_all.16 = f32[16,1,4096]{2,1,0:T(1,128)} all-to-all(f32[16,1,4096]{2,1,0:T(1,128)S(1)} %reshape.12), channel_id=1, replica_groups=mesh['rows'=16,'feat'=16] {'rows'}, dimensions={0} | all-to-all | bytes 524288 | tf_op jit(solution)/shard_map/all_to_all | solution.py:9
  106.4 0.5 broadcast
  106.9 2.2 reduce
  109.1 1.0 reshape.13
  110.2 156.6 %all-reduce.2.cloned.1.call-done = f32[1536,1024]{1,0:T(8,128)} async-done(((f32[1536,1024]{1,0:T(8,128)}), f32[1536,1024]{1,0:T(8,128)}) %all-reduce.2.cloned.1.call-update) | async-done | bytes 6291472 | tf_op jit(solution)/shard_map/psum | solution.py:42
  266.8 0.0 copy-start.1
  266.8 8.0 %convolution_multiply_fusion = f32[1536,64]{0,1:T(8,128)S(1)} fusion(f32[1536,1024]{1,0:T(8,128)} %all-reduce.2.cloned.1.call-done, f32[1024,64]{1,0:T(8,128)} %bitcast.18), kind=kOutput, calls=%fused_computation | convolution fusion | flops 1208057856 | bytes 6946816 | tf_op jit(solution)/shard_map/dot_general | solution.py:45
  274.8 0.0 copy-done.1
  274.8 4.1 %convolution_multiply_fusion.1 = f32[1024,64]{0,1:T(8,128)S(1)} fusion(f32[1536,1024]{1,0:T(8,128)S(1)} %copy-done.1, f32[1536,64]{0,1:T(8,128)S(1)} %convolution_multiply_fusion), kind=kOutput, calls=%fused_computation.1 | convolution fusion | flops 1208025088 | bytes 6946816 | tf_op jit(solution)/shard_map/dot_general | solution.py:54
  279.0 0.9 reshape.11
  279.9 2.0 copy.10
  281.9 1.4 reshape.14
  283.3 27.5 %all_to_all.17 = f32[16,1,4096]{2,1,0:T(1,128)} all-to-all(f32[16,1,4096]{2,1,0:T(1,128)S(1)} %reshape.14), channel_id=1, replica_groups=mesh['rows'=16,'feat'=16] {'rows'}, dimensions={0} | all-to-all | bytes 524288 | tf_op jit(solution)/shard_map/all_to_all | solution.py:31
  310.8 2.2 reduce.1
  313.0 1.0 reshape.15
  314.0 1.1 bitcast_reduce_fusion
  315.1 0.7 copy.7
Async XLA Ops:
  6.5 50.3 %copy-start = (f32[1536,512]{1,0:T(8,128)S(1)}, f32[1536,512]{1,0:T(8,128)}, u32[]{:S(2)}) copy-start(f32[1536,512]{1,0:T(8,128)} %param.3) | copy-start | bytes 9437188
  6.5 260.2 %all-reduce.2.cloned.1.call-start = ((), (), s32[]{:S(2)}) async-start(), calls=%async_computation.3 | async-start | bytes 12582912 | tf_op jit(solution)/shard_map/psum | solution.py:42
  68.9 0.8 copy-start.2
  266.8 8.0 %copy-start.1 = (f32[1536,1024]{1,0:T(8,128)S(1)}, f32[1536,1024]{1,0:T(8,128)}, u32[]{:S(2)}) copy-start(f32[1536,1024]{1,0:T(8,128)} %all-reduce.2.cloned.1.call-done) | copy-start | bytes 18874372
Sparse Core Ops, SparseCore 0:
  69.1 197.6 all-reduce.1
where the time goes:
time: 323 us
  waiting for transfers between devices  157 us (49%)
  blocking collectives  111 us (34%)
  matrix products  24.2 us (7%)
  between operations  13.4 us (4%)
  local copies, waits for them, and re-layouts  11.9 us (4%)
  other arithmetic  5.54 us (2%)
    psum x1, waiting for transfers between devices, on_device(): whitened = lax.psum(partial_y, 'feat')  157 us
    all_to_all x2, blocking collectives, from_everyone(): return lax.all_to_all(copies, axis, split_axis=0, concat_axis=0, tiled=True)  83.5 us
    all_to_all x1, blocking collectives, summed_on_arrival(): tiles = lax.all_to_all(in_blocks(value, dim, peers), axis, 0, 0, tiled=True)  27.5 us
    dot_general x1, matrix products, on_device(): jnp.dot(samples, collect(whitening, 'rows', 1), precision=lax.Precision.H...  12.1 us
    dot_general x1, matrix products, on_device(): jnp.dot(columns, collect(components, 'rows', 0), precision=lax.Precision....  8.02 us
  transfers between devices with their start and end apart: 1, of which 1 were waited for; matrix products, arithmetic and copies ran while one was open for 2% of the time, Pallas kernels for 0%

commit v1 on v0

v1 whole, which is shorter than its diff:
```python
import jax
import jax.numpy as jnp
from jax import lax
from jax.experimental import pallas as pl
from jax.experimental.pallas import tpu as pltpu
from jax.sharding import PartitionSpec as P

MESH = pl.DeviceIdType.MESH
F32 = jnp.float32
BF16 = jnp.bfloat16
NX, NY, NZH, NZL, NC = 4, 4, 2, 4, 2
NZ = NZH * NZL
CH = NY * NZH
ROWS_DEV = 1536
BLK = ROWS_DEV // NX
HB = BLK // 2
SL = BLK // NZL
FD = 512


def split(v):
    hi = v.astype(BF16)
    return hi, (v - hi.astype(F32)).astype(BF16)


def nt(a, b):
    return lax.dot_general(a, b, (((1,), (1,)), ((), ())), preferred_element_type=F32)


def nn(a, b):
    return lax.dot_general(a, b, (((1,), (0,)), ((), ())), preferred_element_type=F32)


def three(dot, ah, al, bh, bl):
    return dot(ah, bh) + (dot(ah, bl) + dot(al, bh))


def kernel(
    s_hbm, w_hbm, c_hbm, out_hbm,
    sv, wv, cv, shi, slo, wall, whi, wlo,
    far, near, own, fr, nr, zb, zr, av, ahi, alo,
    ctp, cx, ct, chi, clo, pt, qhi, qlo, mb, mp, ms, mr, fs, frec, gv, gr, ov, ot, of,
    lsem, wsend, wrecv, wpsend, wprecv, xsend, xrecv, zsend, zrecv, ysend, yrecv,
    csend, crecv, rsend, rrecv, psend, precv, msend, mrecv, fsend, frecv,
):
    i, j = lax.axis_index("rows"), lax.axis_index("feat")
    y, zh, c = i // 4, (i // 2) % 2, i % 2
    zl, x = j // 4, j % 4
    z = zh * 4 + zl
    xl, xr = (x + 3) % 4, (x + 1) % 4

    def dev(y_=None, zh_=None, c_=None, zl_=None, x_=None):
        y_ = y if y_ is None else y_
        zh_ = zh if zh_ is None else zh_
        c_ = c if c_ is None else c_
        zl_ = zl if zl_ is None else zl_
        x_ = x if x_ is None else x_
        return (y_ * 4 + zh_ * 2 + c_, zl_ * 4 + x_)

    def devz(z_, **kw):
        return dev(zh_=z_ // 4, zl_=z_ % 4, **kw)

    def rc(src, dst, ss, rs, to):
        return pltpu.make_async_remote_copy(
            src_ref=src, dst_ref=dst, send_sem=ss, recv_sem=rs, device_id=to, device_id_type=MESH
        )

    def chunk(y_, t):
        u = t % 4
        dy = u + (u // 2) * (1 - 2 * (u % 2))
        return ((y_ + dy) % 4) * 2 + (zh + t // 4) % 2

    wcopy = pltpu.make_async_copy(w_hbm, wv, lsem.at[0])
    ccopy = pltpu.make_async_copy(c_hbm, cv, lsem.at[1])
    wcopy.start()

    def scopy(d):
        rows = pl.ds(pl.multiple_of(((x + d) % 4) * BLK, BLK), BLK)
        return pltpu.make_async_copy(s_hbm.at[rows], sv.at[rows], lsem.at[2 + d])

    for d in (2, 1, 3, 0):
        scopy(d).start()
    ccopy.start()

    barrier = pltpu.get_barrier_semaphore()
    partners = [dev(x_=(x + d) % 4) for d in (1, 2, 3)]
    partners += [dev(y_=(y + d) % 4) for d in (1, 2, 3)]
    partners += [dev(zl_=(zl + d) % 4) for d in (1, 2, 3)]
    partners += [dev(zh_=1 - zh), dev(c_=1 - c), devz((z + 1) % 8), devz((z + 7) % 8)]
    partners += [dev(y_=zl, zl_=y, x_=d) for d in range(4)]
    partners += [devz(d, y_=zl) for d in range(8)]
    for p in partners:
        pl.semaphore_signal(barrier, inc=1, device_id=p, device_id_type=MESH)

    wcopy.wait()
    wt = wv[...].T
    q0 = chunk(y, 0)
    wall[q0, c] = wt

    pl.semaphore_wait(barrier, len(partners))

    def wy(base, q, d, t):
        return rc(wall.at[q, c], wall.at[q, c], wsend.at[base + d], wrecv.at[t], dev(y_=(y + d) % 4))

    def wz():
        return rc(wall.at[q0, c], wall.at[q0, c], wsend.at[4], wrecv.at[4], dev(zh_=1 - zh))

    def wp(t):
        q = chunk(y, t)
        return rc(wall.at[q, c], wall.at[q, c], wpsend.at[t], wprecv.at[t], dev(c_=1 - c))

    def w_arrived(t):
        q = chunk(y, t)
        rc(wall.at[q, c], wall.at[q, c], wsend.at[0], wrecv.at[t], dev(c_=1 - c)).wait_recv()

    def wp_arrived(t):
        q = chunk(y, t)
        rc(wall.at[q, c], wall.at[q, 1 - c], wpsend.at[t], wprecv.at[t], dev(c_=1 - c)).wait_recv()

    wp(0).start()
    wy(0, q0, 3, 1).start()
    wy(0, q0, 1, 2).start()
    wy(0, q0, 2, 3).start()
    wz().start()

    def split_s(d):
        scopy(d).wait()

        def body(n, _):
            rows = pl.ds(pl.multiple_of(((x + d) % 4) * BLK + n * 96, 96), 96)
            h, l = split(sv[rows, :])
            shi[rows, :] = h
            slo[rows, :] = l
            return 0

        lax.fori_loop(0, BLK // 96, body, 0)

    split_s(2)

    ccopy.wait()
    ct_own = cv[...].T
    cz = jnp.zeros((64, 64), F32)
    at0 = jnp.concatenate([ct_own, cz], axis=1)
    at1 = jnp.concatenate([cz, ct_own], axis=1)
    ctp[...] = jnp.where(c == 0, at0, at1).reshape(2, 32, 128)

    def c_swap():
        return rc(ctp.at[1 - c], cx, csend.at[0], crecv.at[0], dev(c_=1 - c))

    c_swap().start()
    qc = zl * 2 + zh

    def c_out(d):
        return rc(ctp.at[c], ct.at[c, y * 2 + zh, x], csend.at[1 + d], crecv.at[1 + x], dev(y_=zl, zl_=y, x_=d))

    def c_keep():
        return pltpu.make_async_copy(ctp.at[c], ct.at[c, y * 2 + zh, x], lsem.at[6])

    def c_in(d):
        return rc(ctp.at[c], ct.at[c, qc, d], csend.at[1 + d], crecv.at[1 + d], dev(y_=zl, zl_=y, x_=d))

    diagonal = y == zl

    def unit(z_):
        return ((z_ % 4) * 2 + z_ // 4) % 8

    def ring_r(k):
        q = unit((z + 9 - k) % 8)
        return rc(ct.at[c, q], ct.at[c, q], rsend.at[0, k], rrecv.at[0, k], devz((z + 1) % 8))

    def ring_l(k):
        q = unit((z + k + 7) % 8)
        return rc(ct.at[c, q], ct.at[c, q], rsend.at[1, k], rrecv.at[1, k], devz((z + 7) % 8))

    def ring_r_in(k):
        q = unit((z + 8 - k) % 8)
        return rc(ct.at[c, q], ct.at[c, q], rsend.at[0, k], rrecv.at[0, k], devz((z + 7) % 8))

    def ring_l_in(k):
        q = unit((z + k) % 8)
        return rc(ct.at[c, q], ct.at[c, q], rsend.at[1, k], rrecv.at[1, k], devz((z + 1) % 8))

    def c_pair():
        return rc(ct.at[c], ct.at[c], psend.at[0], precv.at[0], dev(c_=1 - c))

    def c_pair_in():
        return rc(ct.at[1 - c], ct.at[1 - c], psend.at[0], precv.at[0], dev(c_=1 - c))

    def block(t, d, half):
        rows = pl.ds(pl.multiple_of(((x + d) % 4) * BLK + half * HB, HB), HB)
        return three(nt, shi[rows, :], slo[rows, :], whi[t], wlo[t])

    def x_copy(t, m):
        src, dst, to = (
            (far.at[t, 0], fr.at[t, 0], xr),
            (far.at[t, 1], fr.at[t, 1], xl),
            (near.at[t, 0, 1], nr.at[t, 0, 1], xr),
            (near.at[t, 1, 0], nr.at[t, 1, 0], xl),
            (near.at[t, 0, 0], nr.at[t, 0, 0], xr),
            (near.at[t, 1, 1], nr.at[t, 1, 1], xl),
        )[m]
        return rc(src, dst, xsend.at[t, m], xrecv.at[t, m], dev(x_=to))

    def z_copy(t, d):
        return rc(zb.at[t, (zl + d) % 4], zr.at[t, d - 1], zsend.at[t, d - 1], zrecv.at[t, d - 1], dev(zl_=(zl + d) % 4))

    def y_copy(t, d):
        q = chunk(y, t)
        return rc(av.at[q, y], av.at[q, y], ysend.at[t, d - 1], yrecv.at[t, d - 1], dev(y_=(y + d) % 4))

    def y_in(t, d):
        yo = (y + 4 - d) % 4
        q = chunk(yo, t)
        return rc(av.at[q, yo], av.at[q, yo], ysend.at[t, d - 1], yrecv.at[t, d - 1], dev(y_=yo))

    def far_step(t):
        q = chunk(y, t)
        h, l = split(wall[q].reshape(128, FD))
        whi[t] = h
        wlo[t] = l
        for half in range(2):
            far[t, half] = block(t, 2, half)
            x_copy(t, half).start()

    def near_step(t):
        near[t, 0, 1] = block(t, 1, 1)
        x_copy(t, 2).start()
        near[t, 1, 0] = block(t, 3, 0)
        x_copy(t, 3).start()
        near[t, 0, 0] = block(t, 1, 0)
        near[t, 1, 1] = block(t, 3, 1)

    def join_step(t):
        for side in range(2):
            x_copy(t, side).wait_recv()
            near[t, side, side] = near[t, side, side] + fr[t, side]
            x_copy(t, 4 + side).start()

    def own_step(t):
        for half in range(2):
            own[t, half] = block(t, 0, half)

    def x_finish(t):
        for m in range(2, 6):
            x_copy(t, m).wait_recv()
        for half in range(2):
            v = own[t, half] + nr[t, 0, half] + nr[t, 1, half]
            zb[t, 2 * half] = v[:SL]
            zb[t, 2 * half + 1] = v[SL:]
        for d in (2, 1, 3):
            z_copy(t, d).start()

    def keep(q, yo):
        h, l = split(av[q, yo])
        rows = pl.ds(pl.multiple_of(yo * SL, SL), SL)
        cols = pl.ds(pl.multiple_of(q * 128, 128), 128)
        ahi[rows, cols] = h
        alo[rows, cols] = l

    def z_finish(t):
        for d in (1, 2, 3):
            z_copy(t, d).wait_recv()
        q = chunk(y, t)
        av[q, y] = (zb[t, zl] + zr[t, 0]) + (zr[t, 1] + zr[t, 2])
        for d in (2, 1, 3):
            y_copy(t, d).start()
        keep(q, y)

    def y_finish(t):
        for d in (1, 2, 3):
            y_in(t, d).wait_recv()
            yo = (y + 4 - d) % 4
            keep(chunk(yo, t), yo)

    wp_arrived(0)
    far_step(0)
    for d in (1, 3, 0):
        split_s(d)

    def step(t, _):
        near_step(t)

        @pl.when((t < 7) & (t != 3))
        def _():
            w_arrived(t + 1)
            wp(t + 1).start()

        @pl.when(t == 2)
        def _():
            w_arrived(4)
            q = chunk(y, 4)
            wp(4).start()
            wy(4, q, 3, 5).start()
            wy(4, q, 1, 6).start()
            wy(4, q, 2, 7).start()

        join_step(t)

        @pl.when(t < 7)
        def _():
            wp_arrived(t + 1)
            far_step(t + 1)

        @pl.when(t == 0)
        def _():
            c_swap().wait()
            ctp[c] = ctp[c] + cx[...]
            for d in range(4):

                @pl.when(jnp.logical_not(diagonal & (x == d)))
                def _(d=d):
                    c_out(d).start()

            @pl.when(diagonal)
            def _():
                c_keep().start()
                c_keep().wait()

        @pl.when(t == 1)
        def _():
            for d in range(4):

                @pl.when(jnp.logical_not(diagonal & (x == d)))
                def _(d=d):
                    c_in(d).wait_recv()
                    c_out(d).wait_send()

            ring_r(1).start()
            ring_l(1).start()

        @pl.when((t >= 2) & (t < 6))
        def _():
            ring_r_in(t - 1).wait_recv()
            ring_r(t - 1).wait_send()

        @pl.when((t >= 2) & (t < 5))
        def _():
            ring_r(t).start()
            ring_l_in(t - 1).wait_recv()
            ring_l(t - 1).wait_send()

        @pl.when((t >= 2) & (t < 4))
        def _():
            ring_l(t).start()

        @pl.when(t == 5)
        def _():
            c_pair().start()

        own_step(t)

        @pl.when(t >= 1)
        def _():
            x_finish(t - 1)

        @pl.when(t >= 2)
        def _():
            z_finish(t - 2)

        @pl.when(t >= 3)
        def _():
            y_finish(t - 3)

        return 0

    lax.fori_loop(0, CH, step, 0)
    x_finish(7)
    z_finish(6)
    y_finish(5)

    c_pair().wait_send()
    c_pair_in().wait_recv()

    def split_c(n, _):
        half, q = n // 8, n % 8
        h, l = split(ct[half, q].reshape(128, 128))
        cols = pl.ds(pl.multiple_of(q * 128, 128), 128)
        chi[half, :, cols] = h
        clo[half, :, cols] = l
        return 0

    lax.fori_loop(0, 16, split_c, 0)

    z_finish(7)
    y_finish(6)
    y_finish(7)

    for half in range(2):
        v = three(nt, chi[half], clo[half], ahi[...], alo[...])
        h, l = split(v * v)
        qhi[half] = h
        qlo[half] = l

    def moment_half(half):
        qh, ql = qhi[half], qlo[half]

        def body(n, _):
            cols = pl.ds(pl.multiple_of(n * 256, 256), 256)
            v = three(nn, qh, ql, ahi[:, cols], alo[:, cols])
            for u in range(2):
                mb[half, :, 2 * n + u] = v[:, 128 * u : 128 * u + 128].reshape(4, 32, 128)
            return 0

        lax.fori_loop(0, 4, body, 0)

    def m_pair():
        return rc(mb.at[1 - c], mp, psend.at[1], precv.at[1], dev(c_=1 - c))

    moment_half(1 - c)
    m_pair().start()
    moment_half(c)
    m_pair().wait_recv()

    def m_copy(d):
        return rc(ms.at[(x + d) % 4], mr.at[d - 1], msend.at[d], mrecv.at[d], dev(x_=(x + d) % 4))

    for d in (2, 1, 3, 0):
        b = (x + d) % 4
        ms[b] = mb[c, b] + mp[b]
        if d:
            m_copy(d).start()
    for d in (1, 2, 3):
        m_copy(d).wait_recv()
    fs[...] = (ms[x] + mr[0]) + (mr[1] + mr[2])

    def f_out(q):
        return rc(fs.at[q], frec.at[z], fsend.at[q], frecv.at[z], dev(y_=q // 2, zh_=q % 2, zl_=y))

    def f_in(z_):
        return rc(fs.at[0], frec.at[z_], fsend.at[0], frecv.at[z_], devz(z_, y_=zl))

    mine = y * 2 + zh
    for q in range(8):

        @pl.when(jnp.logical_not(diagonal & (q == mine)))
        def _(q=q):
            f_out(q).start()

    @pl.when(diagonal)
    def _():
        frec[z] = fs[mine]

    for z_ in range(8):

        @pl.when(jnp.logical_not(diagonal & (z == z_)))
        def _(z_=z_):
            f_in(z_).wait_recv()

    total = frec[0]
    for z_ in range(1, 8):
        total = total + frec[z_]
    gv[...] = total * (1.0 / 24576.0**0.5)
    swap = rc(gv, gr, psend.at[2], precv.at[2], dev(c_=1 - c))
    swap.start()
    ov[pl.ds(pl.multiple_of(c * 32, 32), 32), :] = gv[...]
    swap.wait_recv()
    ov[pl.ds(pl.multiple_of((1 - c) * 32, 32), 32), :] = gr[...]
    ot[...] = ov[...].T
    of[...] = ot[pl.ds(pl.multiple_of(c * 64, 64), 64), :]
    result = pltpu.make_async_copy(of, out_hbm, lsem.at[7])
    result.start()

    swap.wait_send()
    m_pair().wait_send()
    for d in (1, 2, 3):
        m_copy(d).wait_send()
        wy(0, q0, d, d).wait_send()
        wy(4, chunk(y, 4), d, d).wait_send()
    wz().wait_send()
    for q in range(8):

        @pl.when(jnp.logical_not(diagonal & (q == mine)))
        def _(q=q):
            f_out(q).wait_send()

    def drain(t, _):
        wp(t).wait_send()
        for m in range(6):
            x_copy(t, m).wait_send()
        for d in (1, 2, 3):
            z_copy(t, d).wait_send()
            y_copy(t, d).wait_send()
        return 0

    lax.fori_loop(0, CH, drain, 0)
    result.wait()


def on_device(samples, whitening, components):
    V = pltpu.VMEM
    D = pltpu.SemaphoreType.DMA
    scratch = [
        V((ROWS_DEV, FD), F32), V((FD, 64), F32), V((64, 64), F32),
        V((ROWS_DEV, FD), BF16), V((ROWS_DEV, FD), BF16),
        V((CH, NC, 64, FD), F32), V((CH, 128, FD), BF16), V((CH, 128, FD), BF16),
        V((CH, 2, HB, 128), F32), V((CH, 2, 2, HB, 128), F32), V((CH, 2, HB, 128), F32),
        V((CH, 2, HB, 128), F32), V((CH, 2, 2, HB, 128), F32),
        V((CH, 4, SL, 128), F32), V((CH, 3, SL, 128), F32),
        V((CH, NY, SL, 128), F32), V((BLK, 1024), BF16), V((BLK, 1024), BF16),
        V((2, 32, 128), F32), V((32, 128), F32), V((2, 8, 4, 32, 128), F32),
        V((2, 128, 1024), BF16), V((2, 128, 1024), BF16),
        V((8, 128), F32), V((2, 128, BLK), BF16), V((2, 128, BLK), BF16),
        V((2, 4, 8, 32, 128), F32), V((4, 8, 32, 128), F32), V((4, 8, 32, 128), F32),
        V((3, 8, 32, 128), F32), V((8, 32, 128), F32), V((8, 32, 128), F32),
        V((32, 128), F32), V((32, 128), F32), V((64, 128), F32), V((128, 64), F32), V((64, 64), F32),
        D((8,)), D((8,)), D((8,)), D((8,)), D((8,)),
        D((8, 6)), D((8, 6)), D((8, 3)), D((8, 3)), D((8, 3)), D((8, 3)),
        D((5,)), D((5,)), D((2, 5)), D((2, 5)), D((3,)), D((3,)), D((4,)), D((4,)), D((8,)), D((8,)),
    ]
    return pl.pallas_call(
        kernel,
        out_shape=jax.ShapeDtypeStruct((64, 64), F32),
        in_specs=[pl.BlockSpec(memory_space=pl.ANY)] * 3,
        out_specs=pl.BlockSpec(memory_space=pl.ANY),
        scratch_shapes=scratch,
        compiler_params=pltpu.CompilerParams(
            collective_id=0, has_side_effects=True, vmem_limit_bytes=60 * 1024 * 1024
        ),
    )(samples, whitening, components)


def solution(mesh):
    placed = (P("rows", "feat"), P("feat", "rows"), P("rows", "feat"))
    return jax.shard_map(
        on_device, mesh=mesh, in_specs=placed, out_specs=P("rows", "feat"), check_vma=False
    )
```

time: 323 us -> 106 us (0.33)
  waiting for transfers between devices: 157 us -> 0 us
  blocking collectives: 111 us -> 0 us
  Pallas kernels: 0 us -> 103 us
  matrix products: 24.2 us -> 0 us
  between operations: 13.4 us -> 0.01 us
  local copies, waits for them, and re-layouts: 11.9 us -> 3.1 us
  other arithmetic: 5.54 us -> 0 us
    psum x1 -> x0, waiting for transfers between devices: 157 us -> none  [on_device(): whitened = lax.psum(partial_y, 'feat')]
    all_to_all x3 -> x0, blocking collectives: 111 us -> none  [the longest x2 83.5 us: from_everyone(): return lax.all_to_all(copies, axis, split_axis=0, concat_axis=0, tiled=True)]
    pallas_call x0 -> x1, Pallas kernels: none -> 103 us  [on_device(): pl.pallas_call(kernel, out_shape=jax.ShapeDtypeStruct((64, 64), F32), in_...]
    dot_general x3 -> x0, matrix products: 24.2 us -> none  [the longest x1 12.1 us: on_device(): jnp.dot(samples, collect(whitening, 'rows', 1), precision=lax.Precision.H...]
    all_to_all x2 -> x0, other arithmetic: 4.45 us -> none  [the longest x1 2.23 us: from_everyone(): return lax.all_to_all(copies, axis, split_axis=0, concat_axis=0, tiled=True)]
  transfers between devices with their start and end apart: 1 -> 0, of which waited for: 1 -> 0; matrix products, arithmetic and copies ran while one was open for 2% -> 0% of each run, Pallas kernels for 0% -> 0%
where the time goes in v1:
time: 106 us
  Pallas kernels  103 us (97%)
  local copies, waits for them, and re-layouts  3.1 us (3%)
    pallas_call x1, Pallas kernels, on_device(): pl.pallas_call(kernel, out_shape=jax.ShapeDtypeStruct((64, 64), F32), in_...  103 us
    unnamed x2, local copies, waits for them, and re-layouts  3.1 us

profile of v1, /device:TPU:1, one launch (start us, length us, event | category | flops | bytes accessed | tf_op | source)
XLA Modules:
  0.0 105.9 jit_solution(18123209154495494082)
XLA Ops:
  0.0 1.7 %copy.4.w_hbm = f32[512,64]{1,0:T(8,128)} copy(f32[512,64]{0,1:T(8,128)} %param.4) | data formatting | bytes 262144 | tf_op args[1]
  1.7 102.7 %shard_map.37 = f32[64,64]{1,0:T(8,128)} custom-call(f32[1536,512]{1,0:T(8,128)} %s_hbm.1, f32[512,64]{1,0:T(8,128)} %copy.4.w_hbm, f32[64,64]{1,0:T(8,128)} %c_hbm.1), custom_call_target="tpu_custom_call" | custom-call | tf_op jit(solution)/shard_map/pallas_call | solution.py:510
  104.5 1.4 %copy.6 = f32[64,64]{1,0:T(8,128)} copy(f32[64,64]{1,0:T(8,128)} %shard_map.37) | data formatting | bytes 32768

commit v2 on v1

--- a/solution.py
+++ b/solution.py
@@ -37,9 +37,9 @@
 
 def kernel(
     s_hbm, w_hbm, c_hbm, out_hbm,
-    sv, wv, cv, shi, slo, wall, whi, wlo,
+    sv, cv, shi, slo, wall, whi, wlo,
     far, near, own, fr, nr, zb, zr, av, ahi, alo,
-    ctp, cx, ct, chi, clo, pt, qhi, qlo, mb, mp, ms, mr, fs, frec, gv, gr, ov, ot, of,
+    ctp, cx, ct, chi, clo, pt, qhi, qlo, mb, mp, ms, mf, mr, fs, frec, gv, gr, ov, ot, of,
     lsem, wsend, wrecv, wpsend, wprecv, xsend, xrecv, zsend, zrecv, ysend, yrecv,
     csend, crecv, rsend, rrecv, psend, precv, msend, mrecv, fsend, frecv,
 ):
@@ -70,7 +70,8 @@
         dy = u + (u // 2) * (1 - 2 * (u % 2))
         return ((y_ + dy) % 4) * 2 + (zh + t // 4) % 2
 
-    wcopy = pltpu.make_async_copy(w_hbm, wv, lsem.at[0])
+    q0 = chunk(y, 0)
+    wcopy = pltpu.make_async_copy(w_hbm, wall.at[q0, c], lsem.at[0])
     ccopy = pltpu.make_async_copy(c_hbm, cv, lsem.at[1])
     wcopy.start()
 
@@ -93,10 +94,6 @@
         pl.semaphore_signal(barrier, inc=1, device_id=p, device_id_type=MESH)
 
     wcopy.wait()
-    wt = wv[...].T
-    q0 = chunk(y, 0)
-    wall[q0, c] = wt
-
     pl.semaphore_wait(barrier, len(partners))
 
     def wy(base, q, d, t):
@@ -186,8 +183,8 @@
     def c_pair_in():
         return rc(ct.at[1 - c], ct.at[1 - c], psend.at[0], precv.at[0], dev(c_=1 - c))
 
-    def block(t, d, half):
-        rows = pl.ds(pl.multiple_of(((x + d) % 4) * BLK + half * HB, HB), HB)
+    def block(t, d):
+        rows = pl.ds(pl.multiple_of(((x + d) % 4) * BLK, BLK), BLK)
         return three(nt, shi[rows, :], slo[rows, :], whi[t], wlo[t])
 
     def x_copy(t, m):
@@ -215,20 +212,24 @@
 
     def far_step(t):
         q = chunk(y, t)
-        h, l = split(wall[q].reshape(128, FD))
-        whi[t] = h
-        wlo[t] = l
-        for half in range(2):
-            far[t, half] = block(t, 2, half)
-            x_copy(t, half).start()
+
+        def body(n, _):
+            h, l = split(wall[q, n])
+            rows = pl.ds(pl.multiple_of(n * 64, 64), 64)
+            whi[t, rows, :] = h
+            wlo[t, rows, :] = l
+            return 0
+
+        lax.fori_loop(0, NC, body, 0)
+        far[t] = block(t, 2).reshape(2, HB, 128)
+        x_copy(t, 0).start()
+        x_copy(t, 1).start()
 
     def near_step(t):
-        near[t, 0, 1] = block(t, 1, 1)
+        near[t, 0] = block(t, 1).reshape(2, HB, 128)
         x_copy(t, 2).start()
-        near[t, 1, 0] = block(t, 3, 0)
+        near[t, 1] = block(t, 3).reshape(2, HB, 128)
         x_copy(t, 3).start()
-        near[t, 0, 0] = block(t, 1, 0)
-        near[t, 1, 1] = block(t, 3, 1)
 
     def join_step(t):
         for side in range(2):
@@ -237,8 +238,7 @@
             x_copy(t, 4 + side).start()
 
     def own_step(t):
-        for half in range(2):
-            own[t, half] = block(t, 0, half)
+        own[t] = block(t, 0).reshape(2, HB, 128)
 
     def x_finish(t):
         for m in range(2, 6):
@@ -252,7 +252,7 @@
 
     def keep(q, yo):
         h, l = split(av[q, yo])
-        rows = pl.ds(pl.multiple_of(yo * SL, SL), SL)
+        rows = pl.ds(pl.multiple_of(yo * 128, 128), SL)
         cols = pl.ds(pl.multiple_of(q * 128, 128), 128)
         ahi[rows, cols] = h
         alo[rows, cols] = l
@@ -272,6 +272,9 @@
             yo = (y + 4 - d) % 4
             keep(chunk(yo, t), yo)
 
+    for slot in range(NY):
+        ahi[128 * slot + SL : 128 * slot + 128, :] = jnp.zeros((128 - SL, 1024), BF16)
+        alo[128 * slot + SL : 128 * slot + 128, :] = jnp.zeros((128 - SL, 1024), BF16)
     wp_arrived(0)
     far_step(0)
     for d in (1, 3, 0):
@@ -280,16 +283,19 @@
     def step(t, _):
         near_step(t)
 
-        @pl.when((t < 7) & (t != 3))
-        def _():
-            w_arrived(t + 1)
-            wp(t + 1).start()
+        @pl.when(t == 0)
+        def _():
+            w_arrived(1)
+            wp(1).start()
+
+        @pl.when(t < 6)
+        def _():
+            w_arrived(t + 2)
+            wp(t + 2).start()
 
         @pl.when(t == 2)
         def _():
-            w_arrived(4)
             q = chunk(y, 4)
-            wp(4).start()
             wy(4, q, 3, 5).start()
             wy(4, q, 1, 6).start()
             wy(4, q, 2, 7).start()
@@ -316,7 +322,7 @@
                 c_keep().start()
                 c_keep().wait()
 
-        @pl.when(t == 1)
+        @pl.when(t == 2)
         def _():
             for d in range(4):
 
@@ -328,22 +334,22 @@
             ring_r(1).start()
             ring_l(1).start()
 
-        @pl.when((t >= 2) & (t < 6))
-        def _():
-            ring_r_in(t - 1).wait_recv()
-            ring_r(t - 1).wait_send()
-
-        @pl.when((t >= 2) & (t < 5))
-        def _():
-            ring_r(t).start()
-            ring_l_in(t - 1).wait_recv()
-            ring_l(t - 1).wait_send()
-
-        @pl.when((t >= 2) & (t < 4))
-        def _():
-            ring_l(t).start()
-
-        @pl.when(t == 5)
+        @pl.when((t >= 3) & (t < 7))
+        def _():
+            ring_r_in(t - 2).wait_recv()
+            ring_r(t - 2).wait_send()
+
+        @pl.when((t >= 3) & (t < 6))
+        def _():
+            ring_r(t - 1).start()
+            ring_l_in(t - 2).wait_recv()
+            ring_l(t - 2).wait_send()
+
+        @pl.when((t >= 3) & (t < 5))
+        def _():
+            ring_l(t - 1).start()
+
+        @pl.when(t == 6)
         def _():
             c_pair().start()
 
@@ -353,75 +359,115 @@
         def _():
             x_finish(t - 1)
 
-        @pl.when(t >= 2)
-        def _():
-            z_finish(t - 2)
-
         @pl.when(t >= 3)
         def _():
-            y_finish(t - 3)
+            z_finish(t - 3)
+
+        @pl.when(t >= 5)
+        def _():
+            y_finish(t - 5)
 
         return 0
 
     lax.fori_loop(0, CH, step, 0)
+    z_finish(5)
     x_finish(7)
+    y_finish(3)
     z_finish(6)
-    y_finish(5)
+    y_finish(4)
 
     c_pair().wait_send()
     c_pair_in().wait_recv()
 
-    def split_c(n, _):
-        half, q = n // 8, n % 8
-        h, l = split(ct[half, q].reshape(128, 128))
+    def split_c(q, _):
         cols = pl.ds(pl.multiple_of(q * 128, 128), 128)
-        chi[half, :, cols] = h
-        clo[half, :, cols] = l
+        for half in range(2):
+            h, l = split(ct[half, q].reshape(128, 128))
+            chi[128 * half : 128 * half + 128, cols] = h
+            clo[128 * half : 128 * half + 128, cols] = l
         return 0
 
-    lax.fori_loop(0, 16, split_c, 0)
-
+    lax.fori_loop(0, 8, split_c, 0)
+    y_finish(5)
+
+    def project(t, d):
+        yo = (y + 4 - d) % 4
+        cols = pl.ds(pl.multiple_of(chunk(yo, t) * 128, 128), 128)
+        slot = pl.ds(pl.multiple_of(yo * 128, 128), 128)
+        pt[:, slot] = pt[:, slot] + three(nt, chi[:, cols], clo[:, cols], ahi[slot, cols], alo[slot, cols])
+
+    def project_some(n, _):
+        project(n // 4, n % 4)
+        return 0
+
+    pt[...] = jnp.zeros_like(pt)
+    lax.fori_loop(0, 24, project_some, 0)
     z_finish(7)
     y_finish(6)
+    lax.fori_loop(24, 29, project_some, 0)
     y_finish(7)
-
-    for half in range(2):
-        v = three(nt, chi[half], clo[half], ahi[...], alo[...])
-        h, l = split(v * v)
-        qhi[half] = h
-        qlo[half] = l
-
-    def moment_half(half):
-        qh, ql = qhi[half], qlo[half]
-
+    lax.fori_loop(29, 32, project_some, 0)
+
+    h, l = split(pt[...] * pt[...])
+    qhi[...] = h.reshape(2, 128, 512)
+    qlo[...] = l.reshape(2, 128, 512)
+
+    def moment_part(half, part):
         def body(n, _):
-            cols = pl.ds(pl.multiple_of(n * 256, 256), 256)
-            v = three(nn, qh, ql, ahi[:, cols], alo[:, cols])
+            cols = pl.ds(pl.multiple_of(part * 512 + n * 256, 256), 256)
+            v = three(nn, qhi[half], qlo[half], ahi[:, cols], alo[:, cols])
             for u in range(2):
-                mb[half, :, 2 * n + u] = v[:, 128 * u : 128 * u + 128].reshape(4, 32, 128)
+                mb[half, part, :, 2 * n + u] = v[:, 128 * u : 128 * u + 128].reshape(4, 32, 128)
             return 0
 
-        lax.fori_loop(0, 4, body, 0)
-
-    def m_pair():
-        return rc(mb.at[1 - c], mp, psend.at[1], precv.at[1], dev(c_=1 - c))
-
-    moment_half(1 - c)
-    m_pair().start()
-    moment_half(c)
-    m_pair().wait_recv()
-
-    def m_copy(d):
-        return rc(ms.at[(x + d) % 4], mr.at[d - 1], msend.at[d], mrecv.at[d], dev(x_=(x + d) % 4))
-
-    for d in (2, 1, 3, 0):
-        b = (x + d) % 4
-        ms[b] = mb[c, b] + mp[b]
-        if d:
-            m_copy(d).start()
-    for d in (1, 2, 3):
-        m_copy(d).wait_recv()
-    fs[...] = (ms[x] + mr[0]) + (mr[1] + mr[2])
+        lax.fori_loop(0, 2, body, 0)
+
+    def m_pair(part):
+        return rc(mb.at[1 - c, part], mp.at[part], psend.at[1 + part], precv.at[1 + part], dev(c_=1 - c))
+
+    for part in range(2):
+        moment_part(1 - c, part)
+        m_pair(part).start()
+    for part in range(2):
+        moment_part(c, part)
+
+    def m_copy(m):
+        src, dst, to = (
+            (ms.at[(x + 2) % 4, 0], mf.at[0], xr),
+            (ms.at[(x + 2) % 4, 1], mf.at[1], xl),
+            (ms.at[xr, 1], mr.at[0, 1], xr),
+            (ms.at[xl, 0], mr.at[1, 0], xl),
+            (ms.at[xr, 0], mr.at[0, 0], xr),
+            (ms.at[xl, 1], mr.at[1, 1], xl),
+        )[m]
+        return rc(src, dst, msend.at[m], mrecv.at[m], dev(x_=to))
+
+    def m_sum(b, part):
+        ms[b, part] = mb[c, part, b] + mp[part, b]
+
+    m_pair(0).wait_recv()
+    m_sum((x + 2) % 4, 0)
+    m_copy(0).start()
+    m_sum(xl, 0)
+    m_copy(3).start()
+    m_pair(1).wait_recv()
+    m_sum((x + 2) % 4, 1)
+    m_copy(1).start()
+    m_sum(xr, 1)
+    m_copy(2).start()
+    m_sum(xr, 0)
+    m_copy(0).wait_recv()
+    ms[xr, 0] = ms[xr, 0] + mf[0]
+    m_copy(4).start()
+    m_sum(xl, 1)
+    m_copy(1).wait_recv()
+    ms[xl, 1] = ms[xl, 1] + mf[1]
+    m_copy(5).start()
+    m_sum(x, 0)
+    m_sum(x, 1)
+    for m in range(2, 6):
+        m_copy(m).wait_recv()
+    fs[...] = ms[x].reshape(8, 32, 128) + (mr[0] + mr[1]).reshape(8, 32, 128)
 
     def f_out(q):
         return rc(fs.at[q], frec.at[z], fsend.at[q], frecv.at[z], dev(y_=q // 2, zh_=q % 2, zl_=y))
@@ -450,7 +496,7 @@
     for z_ in range(1, 8):
         total = total + frec[z_]
     gv[...] = total * (1.0 / 24576.0**0.5)
-    swap = rc(gv, gr, psend.at[2], precv.at[2], dev(c_=1 - c))
+    swap = rc(gv, gr, psend.at[3], precv.at[3], dev(c_=1 - c))
     swap.start()
     ov[pl.ds(pl.multiple_of(c * 32, 32), 32), :] = gv[...]
     swap.wait_recv()
@@ -461,9 +507,11 @@
     result.start()
 
     swap.wait_send()
-    m_pair().wait_send()
+    m_pair(0).wait_send()
+    m_pair(1).wait_send()
+    for m in range(6):
+        m_copy(m).wait_send()
     for d in (1, 2, 3):
-        m_copy(d).wait_send()
         wy(0, q0, d, d).wait_send()
         wy(4, chunk(y, 4), d, d).wait_send()
     wz().wait_send()
@@ -490,22 +538,22 @@
     V = pltpu.VMEM
     D = pltpu.SemaphoreType.DMA
     scratch = [
-        V((ROWS_DEV, FD), F32), V((FD, 64), F32), V((64, 64), F32),
+        V((ROWS_DEV, FD), F32), V((64, 64), F32),
         V((ROWS_DEV, FD), BF16), V((ROWS_DEV, FD), BF16),
         V((CH, NC, 64, FD), F32), V((CH, 128, FD), BF16), V((CH, 128, FD), BF16),
         V((CH, 2, HB, 128), F32), V((CH, 2, 2, HB, 128), F32), V((CH, 2, HB, 128), F32),
         V((CH, 2, HB, 128), F32), V((CH, 2, 2, HB, 128), F32),
         V((CH, 4, SL, 128), F32), V((CH, 3, SL, 128), F32),
-        V((CH, NY, SL, 128), F32), V((BLK, 1024), BF16), V((BLK, 1024), BF16),
+        V((CH, NY, SL, 128), F32), V((512, 1024), BF16), V((512, 1024), BF16),
         V((2, 32, 128), F32), V((32, 128), F32), V((2, 8, 4, 32, 128), F32),
-        V((2, 128, 1024), BF16), V((2, 128, 1024), BF16),
-        V((8, 128), F32), V((2, 128, BLK), BF16), V((2, 128, BLK), BF16),
-        V((2, 4, 8, 32, 128), F32), V((4, 8, 32, 128), F32), V((4, 8, 32, 128), F32),
-        V((3, 8, 32, 128), F32), V((8, 32, 128), F32), V((8, 32, 128), F32),
+        V((256, 1024), BF16), V((256, 1024), BF16),
+        V((256, 512), F32), V((2, 128, 512), BF16), V((2, 128, 512), BF16),
+        V((2, 2, 4, 4, 32, 128), F32), V((2, 4, 4, 32, 128), F32), V((4, 2, 4, 32, 128), F32),
+        V((2, 4, 32, 128), F32), V((2, 2, 4, 32, 128), F32), V((8, 32, 128), F32), V((8, 32, 128), F32),
         V((32, 128), F32), V((32, 128), F32), V((64, 128), F32), V((128, 64), F32), V((64, 64), F32),
         D((8,)), D((8,)), D((8,)), D((8,)), D((8,)),
         D((8, 6)), D((8, 6)), D((8, 3)), D((8, 3)), D((8, 3)), D((8, 3)),
-        D((5,)), D((5,)), D((2, 5)), D((2, 5)), D((3,)), D((3,)), D((4,)), D((4,)), D((8,)), D((8,)),
+        D((5,)), D((5,)), D((2, 5)), D((2, 5)), D((4,)), D((4,)), D((6,)), D((6,)), D((8,)), D((8,)),
     ]
     return pl.pallas_call(
         kernel,
@@ -516,7 +564,7 @@
         compiler_params=pltpu.CompilerParams(
             collective_id=0, has_side_effects=True, vmem_limit_bytes=60 * 1024 * 1024
         ),
-    )(samples, whitening, components)
+    )(samples, whitening.T, components)
 
 
 def solution(mesh):

time: 106 us -> 106 us (level)
  Pallas kernels: 103 us -> 105 us
  local copies, waits for them, and re-layouts: 3.1 us -> 1.38 us
    pallas_call x1, Pallas kernels: 103 us -> 105 us  [on_device(): pl.pallas_call(kernel, out_shape=jax.ShapeDtypeStruct((64, 64), F32), in_...]
    unnamed x2 -> x1, local copies, waits for them, and re-layouts: 3.1 us -> 1.38 us
where the time goes in v2:
time: 106 us
  Pallas kernels  105 us (99%)
  local copies, waits for them, and re-layouts  1.38 us (1%)
    pallas_call x1, Pallas kernels, on_device(): pl.pallas_call(kernel, out_shape=jax.ShapeDtypeStruct((64, 64), F32), in_...  105 us

profile of v2, /device:TPU:1, one launch (start us, length us, event | category | flops | bytes accessed | tf_op | source)
XLA Modules:
  0.0 106.1 jit_solution(12735170069762327584)
XLA Ops:
  0.0 104.7 %shard_map.37 = f32[64,64]{1,0:T(8,128)} custom-call(f32[1536,512]{1,0:T(8,128)} %s_hbm.1, f32[64,512]{1,0:T(8,128)} %bitcast.1, f32[64,64]{1,0:T(8,128)} %c_hbm.1), custom_call_target="tpu_custom_call" | custom-call | tf_op jit(solution)/shard_map/pallas_call | solution.py:558
  104.7 1.4 %copy.5 = f32[64,64]{1,0:T(8,128)} copy(f32[64,64]{1,0:T(8,128)} %shard_map.37) | data formatting | bytes 32768

commit v3 on v2

--- a/solution.py
+++ b/solution.py
@@ -13,8 +13,9 @@
 CH = NY * NZH
 ROWS_DEV = 1536
 BLK = ROWS_DEV // NX
-HB = BLK // 2
-SL = BLK // NZL
+ST = 2 * CH
+HB = BLK // 4
+SL = BLK // NZL // 2
 FD = 512
 
 
@@ -41,7 +42,7 @@
     far, near, own, fr, nr, zb, zr, av, ahi, alo,
     ctp, cx, ct, chi, clo, pt, qhi, qlo, mb, mp, ms, mf, mr, fs, frec, gv, gr, ov, ot, of,
     lsem, wsend, wrecv, wpsend, wprecv, xsend, xrecv, zsend, zrecv, ysend, yrecv,
-    csend, crecv, rsend, rrecv, psend, precv, msend, mrecv, fsend, frecv,
+    csend, crecv, rsend, rrecv, psend, precv, msend, mrecv, fsend, frecv, tok_a, tok_b,
 ):
     i, j = lax.axis_index("rows"), lax.axis_index("feat")
     y, zh, c = i // 4, (i // 2) % 2, i % 2
@@ -88,8 +89,6 @@
     partners += [dev(y_=(y + d) % 4) for d in (1, 2, 3)]
     partners += [dev(zl_=(zl + d) % 4) for d in (1, 2, 3)]
     partners += [dev(zh_=1 - zh), dev(c_=1 - c), devz((z + 1) % 8), devz((z + 7) % 8)]
-    partners += [dev(y_=zl, zl_=y, x_=d) for d in range(4)]
-    partners += [devz(d, y_=zl) for d in range(8)]
     for p in partners:
         pl.semaphore_signal(barrier, inc=1, device_id=p, device_id_type=MESH)
 
@@ -119,6 +118,8 @@
     wy(0, q0, 1, 2).start()
     wy(0, q0, 2, 3).start()
     wz().start()
+    for d in (1, 2, 3):
+        pl.semaphore_signal(tok_a, inc=1, device_id=dev(zl_=(zl + d) % 4), device_id_type=MESH)
 
     def split_s(d):
         scopy(d).wait()
@@ -184,8 +185,8 @@
         return rc(ct.at[1 - c], ct.at[1 - c], psend.at[0], precv.at[0], dev(c_=1 - c))
 
     def block(t, d):
-        rows = pl.ds(pl.multiple_of(((x + d) % 4) * BLK, BLK), BLK)
-        return three(nt, shi[rows, :], slo[rows, :], whi[t], wlo[t])
+        rows = pl.ds(pl.multiple_of(((x + d) % 4) * BLK + (t % 2) * 2 * HB, 2 * HB), 2 * HB)
+        return three(nt, shi[rows, :], slo[rows, :], whi[t // 2], wlo[t // 2]).reshape(2, HB, 128)
 
     def x_copy(t, m):
         src, dst, to = (
@@ -202,33 +203,37 @@
         return rc(zb.at[t, (zl + d) % 4], zr.at[t, d - 1], zsend.at[t, d - 1], zrecv.at[t, d - 1], dev(zl_=(zl + d) % 4))
 
     def y_copy(t, d):
-        q = chunk(y, t)
-        return rc(av.at[q, y], av.at[q, y], ysend.at[t, d - 1], yrecv.at[t, d - 1], dev(y_=(y + d) % 4))
+        q = chunk(y, t // 2)
+        h = t % 2
+        return rc(av.at[q, y, h], av.at[q, y, h], ysend.at[t, d - 1], yrecv.at[t, d - 1], dev(y_=(y + d) % 4))
 
     def y_in(t, d):
         yo = (y + 4 - d) % 4
-        q = chunk(yo, t)
-        return rc(av.at[q, yo], av.at[q, yo], ysend.at[t, d - 1], yrecv.at[t, d - 1], dev(y_=yo))
-
-    def far_step(t):
-        q = chunk(y, t)
+        q = chunk(yo, t // 2)
+        h = t % 2
+        return rc(av.at[q, yo, h], av.at[q, yo, h], ysend.at[t, d - 1], yrecv.at[t, d - 1], dev(y_=yo))
+
+    def split_w(tc):
+        q = chunk(y, tc)
 
         def body(n, _):
             h, l = split(wall[q, n])
             rows = pl.ds(pl.multiple_of(n * 64, 64), 64)
-            whi[t, rows, :] = h
-            wlo[t, rows, :] = l
+            whi[tc, rows, :] = h
+            wlo[tc, rows, :] = l
             return 0
 
         lax.fori_loop(0, NC, body, 0)
-        far[t] = block(t, 2).reshape(2, HB, 128)
+
+    def far_step(t):
+        far[t] = block(t, 2)
         x_copy(t, 0).start()
         x_copy(t, 1).start()
 
     def near_step(t):
-        near[t, 0] = block(t, 1).reshape(2, HB, 128)
+        near[t, 0] = block(t, 1)
         x_copy(t, 2).start()
-        near[t, 1] = block(t, 3).reshape(2, HB, 128)
+        near[t, 1] = block(t, 3)
         x_copy(t, 3).start()
 
     def join_step(t):
@@ -238,7 +243,7 @@
             x_copy(t, 4 + side).start()
 
     def own_step(t):
-        own[t] = block(t, 0).reshape(2, HB, 128)
+        own[t] = block(t, 0)
 
     def x_finish(t):
         for m in range(2, 6):
@@ -250,39 +255,39 @@
         for d in (2, 1, 3):
             z_copy(t, d).start()
 
-    def keep(q, yo):
-        h, l = split(av[q, yo])
-        rows = pl.ds(pl.multiple_of(yo * 128, 128), SL)
+    def keep(q, yo, h):
+        hi, lo = split(av[q, yo, h])
+        rows = pl.ds(pl.multiple_of(yo * 128 + h * SL, 16), SL)
         cols = pl.ds(pl.multiple_of(q * 128, 128), 128)
-        ahi[rows, cols] = h
-        alo[rows, cols] = l
+        ahi[rows, cols] = hi
+        alo[rows, cols] = lo
 
     def z_finish(t):
         for d in (1, 2, 3):
             z_copy(t, d).wait_recv()
-        q = chunk(y, t)
-        av[q, y] = (zb[t, zl] + zr[t, 0]) + (zr[t, 1] + zr[t, 2])
+        q = chunk(y, t // 2)
+        h = t % 2
+        av[q, y, h] = (zb[t, zl] + zr[t, 0]) + (zr[t, 1] + zr[t, 2])
         for d in (2, 1, 3):
             y_copy(t, d).start()
-        keep(q, y)
+        keep(q, y, h)
 
     def y_finish(t):
         for d in (1, 2, 3):
             y_in(t, d).wait_recv()
             yo = (y + 4 - d) % 4
-            keep(chunk(yo, t), yo)
+            keep(chunk(yo, t // 2), yo, t % 2)
 
     for slot in range(NY):
-        ahi[128 * slot + SL : 128 * slot + 128, :] = jnp.zeros((128 - SL, 1024), BF16)
-        alo[128 * slot + SL : 128 * slot + 128, :] = jnp.zeros((128 - SL, 1024), BF16)
+        ahi[128 * slot + 2 * SL : 128 * slot + 128, :] = jnp.zeros((128 - 2 * SL, 1024), BF16)
+        alo[128 * slot + 2 * SL : 128 * slot + 128, :] = jnp.zeros((128 - 2 * SL, 1024), BF16)
     wp_arrived(0)
+    split_w(0)
     far_step(0)
     for d in (1, 3, 0):
         split_s(d)
 
-    def step(t, _):
-        near_step(t)
-
+    def whitening_step(t):
         @pl.when(t == 0)
         def _():
             w_arrived(1)
@@ -300,15 +305,16 @@
             wy(4, q, 1, 6).start()
             wy(4, q, 2, 7).start()
 
-        join_step(t)
-
-        @pl.when(t < 7)
-        def _():
-            wp_arrived(t + 1)
-            far_step(t + 1)
-
+    def component_step(t):
         @pl.when(t == 0)
         def _():
+            pl.semaphore_wait(tok_a, 3)
+            for d in (1, 2, 3):
+                pl.semaphore_signal(tok_b, inc=1, device_id=dev(x_=(x + d) % 4), device_id_type=MESH)
+
+        @pl.when(t == 1)
+        def _():
+            pl.semaphore_wait(tok_b, 3)
             c_swap().wait()
             ctp[c] = ctp[c] + cx[...]
             for d in range(4):
@@ -353,28 +359,55 @@
         def _():
             c_pair().start()
 
-        own_step(t)
-
-        @pl.when(t >= 1)
-        def _():
-            x_finish(t - 1)
-
-        @pl.when(t >= 3)
-        def _():
-            z_finish(t - 3)
-
-        @pl.when(t >= 5)
-        def _():
-            y_finish(t - 5)
+    def step(tc, _):
+        for h in range(2):
+            t = 2 * tc + h
+            near_step(t)
+            if h == 0:
+                whitening_step(tc)
+            join_step(t)
+            if h == 0:
+                far_step(t + 1)
+                component_step(tc)
+            else:
+
+                @pl.when(tc < 7)
+                def _():
+                    wp_arrived(tc + 1)
+                    split_w(tc + 1)
+                    far_step(t + 1)
+
+            own_step(t)
+
+            @pl.when(t >= 2)
+            def _():
+                x_finish(t - 2)
+
+            @pl.when(t >= 5)
+            def _():
+                z_finish(t - 5)
+
+            @pl.when(t >= 8)
+            def _():
+                y_finish(t - 8)
 
         return 0
 
+    def finish(what, lo, hi):
+        def body(t, _):
+            what(t)
+            return 0
+
+        lax.fori_loop(lo, hi, body, 0)
+
     lax.fori_loop(0, CH, step, 0)
-    z_finish(5)
-    x_finish(7)
-    y_finish(3)
-    z_finish(6)
-    y_finish(4)
+    z_finish(11)
+    x_finish(14)
+    finish(z_finish, 12, 14)
+    finish(y_finish, 8, 10)
+    x_finish(15)
+    z_finish(14)
+    finish(y_finish, 10, 12)
 
     c_pair().wait_send()
     c_pair_in().wait_recv()
@@ -388,7 +421,6 @@
         return 0
 
     lax.fori_loop(0, 8, split_c, 0)
-    y_finish(5)
 
     def project(t, d):
         yo = (y + 4 - d) % 4
@@ -402,10 +434,11 @@
 
     pt[...] = jnp.zeros_like(pt)
     lax.fori_loop(0, 24, project_some, 0)
-    z_finish(7)
-    y_finish(6)
-    lax.fori_loop(24, 29, project_some, 0)
-    y_finish(7)
+    finish(y_finish, 12, 14)
+    lax.fori_loop(24, 28, project_some, 0)
+    z_finish(15)
+    lax.fori_loop(28, 29, project_some, 0)
+    finish(y_finish, 14, 16)
     lax.fori_loop(29, 32, project_some, 0)
 
     h, l = split(pt[...] * pt[...])
@@ -521,8 +554,13 @@
         def _(q=q):
             f_out(q).wait_send()
 
+    def drain_w(t, _):
+        wp(t).wait_send()
+        return 0
+
+    lax.fori_loop(0, CH, drain_w, 0)
+
     def drain(t, _):
-        wp(t).wait_send()
         for m in range(6):
             x_copy(t, m).wait_send()
         for d in (1, 2, 3):
@@ -530,7 +568,7 @@
             y_copy(t, d).wait_send()
         return 0
 
-    lax.fori_loop(0, CH, drain, 0)
+    lax.fori_loop(0, ST, drain, 0)
     result.wait()
 
 
@@ -541,10 +579,10 @@
         V((ROWS_DEV, FD), F32), V((64, 64), F32),
         V((ROWS_DEV, FD), BF16), V((ROWS_DEV, FD), BF16),
         V((CH, NC, 64, FD), F32), V((CH, 128, FD), BF16), V((CH, 128, FD), BF16),
-        V((CH, 2, HB, 128), F32), V((CH, 2, 2, HB, 128), F32), V((CH, 2, HB, 128), F32),
-        V((CH, 2, HB, 128), F32), V((CH, 2, 2, HB, 128), F32),
-        V((CH, 4, SL, 128), F32), V((CH, 3, SL, 128), F32),
-        V((CH, NY, SL, 128), F32), V((512, 1024), BF16), V((512, 1024), BF16),
+        V((ST, 2, HB, 128), F32), V((ST, 2, 2, HB, 128), F32), V((ST, 2, HB, 128), F32),
+        V((ST, 2, HB, 128), F32), V((ST, 2, 2, HB, 128), F32),
+        V((ST, 4, SL, 128), F32), V((ST, 3, SL, 128), F32),
+        V((CH, NY, 2, SL, 128), F32), V((512, 1024), BF16), V((512, 1024), BF16),
         V((2, 32, 128), F32), V((32, 128), F32), V((2, 8, 4, 32, 128), F32),
         V((256, 1024), BF16), V((256, 1024), BF16),
         V((256, 512), F32), V((2, 128, 512), BF16), V((2, 128, 512), BF16),
@@ -552,8 +590,9 @@
         V((2, 4, 32, 128), F32), V((2, 2, 4, 32, 128), F32), V((8, 32, 128), F32), V((8, 32, 128), F32),
         V((32, 128), F32), V((32, 128), F32), V((64, 128), F32), V((128, 64), F32), V((64, 64), F32),
         D((8,)), D((8,)), D((8,)), D((8,)), D((8,)),
-        D((8, 6)), D((8, 6)), D((8, 3)), D((8, 3)), D((8, 3)), D((8, 3)),
+        D((ST, 6)), D((ST, 6)), D((ST, 3)), D((ST, 3)), D((ST, 3)), D((ST, 3)),
         D((5,)), D((5,)), D((2, 5)), D((2, 5)), D((4,)), D((4,)), D((6,)), D((6,)), D((8,)), D((8,)),
+        pltpu.SemaphoreType.REGULAR, pltpu.SemaphoreType.REGULAR,
     ]
     return pl.pallas_call(
         kernel,

time: 106 us -> 125 us (1.18)
  Pallas kernels: 105 us -> 123 us
    pallas_call x1, Pallas kernels: 105 us -> 123 us  [on_device(): pl.pallas_call(kernel, out_shape=jax.ShapeDtypeStruct((64, 64), F32), in_...]
where the time goes in v3:
time: 125 us
  Pallas kernels  123 us (98%)
  local copies, waits for them, and re-layouts  1.38 us (1%)
    pallas_call x1, Pallas kernels, on_device(): pl.pallas_call(kernel, out_shape=jax.ShapeDtypeStruct((64, 64), F32), in_...  123 us

profile of v3, /device:TPU:1, one launch (start us, length us, event | category | flops | bytes accessed | tf_op | source)
XLA Modules:
  0.0 124.7 jit_solution(11874916366018813292)
XLA Ops:
  0.0 123.3 %shard_map.37 = f32[64,64]{1,0:T(8,128)} custom-call(f32[1536,512]{1,0:T(8,128)} %s_hbm.1, f32[64,512]{1,0:T(8,128)} %bitcast.1, f32[64,64]{1,0:T(8,128)} %c_hbm.1), custom_call_target="tpu_custom_call" | custom-call | tf_op jit(solution)/shard_map/pallas_call | solution.py:597
  123.3 1.4 %copy.5 = f32[64,64]{1,0:T(8,128)} copy(f32[64,64]{1,0:T(8,128)} %shard_map.37) | data formatting | bytes 32768

commit v4 on v2

--- a/solution.py
+++ b/solution.py
@@ -41,7 +41,7 @@
     far, near, own, fr, nr, zb, zr, av, ahi, alo,
     ctp, cx, ct, chi, clo, pt, qhi, qlo, mb, mp, ms, mf, mr, fs, frec, gv, gr, ov, ot, of,
     lsem, wsend, wrecv, wpsend, wprecv, xsend, xrecv, zsend, zrecv, ysend, yrecv,
-    csend, crecv, rsend, rrecv, psend, precv, msend, mrecv, fsend, frecv,
+    csend, crecv, rsend, rrecv, psend, precv, msend, mrecv, fsend, frecv, tok_a, tok_b,
 ):
     i, j = lax.axis_index("rows"), lax.axis_index("feat")
     y, zh, c = i // 4, (i // 2) % 2, i % 2
@@ -88,8 +88,6 @@
     partners += [dev(y_=(y + d) % 4) for d in (1, 2, 3)]
     partners += [dev(zl_=(zl + d) % 4) for d in (1, 2, 3)]
     partners += [dev(zh_=1 - zh), dev(c_=1 - c), devz((z + 1) % 8), devz((z + 7) % 8)]
-    partners += [dev(y_=zl, zl_=y, x_=d) for d in range(4)]
-    partners += [devz(d, y_=zl) for d in range(8)]
     for p in partners:
         pl.semaphore_signal(barrier, inc=1, device_id=p, device_id_type=MESH)
 
@@ -119,6 +117,8 @@
     wy(0, q0, 1, 2).start()
     wy(0, q0, 2, 3).start()
     wz().start()
+    for d in (1, 2, 3):
+        pl.semaphore_signal(tok_a, inc=1, device_id=dev(zl_=(zl + d) % 4), device_id_type=MESH)
 
     def split_s(d):
         scopy(d).wait()
@@ -210,7 +210,7 @@
         q = chunk(yo, t)
         return rc(av.at[q, yo], av.at[q, yo], ysend.at[t, d - 1], yrecv.at[t, d - 1], dev(y_=yo))
 
-    def far_step(t):
+    def split_w(t):
         q = chunk(y, t)
 
         def body(n, _):
@@ -221,6 +221,8 @@
             return 0
 
         lax.fori_loop(0, NC, body, 0)
+
+    def far_step(t):
         far[t] = block(t, 2).reshape(2, HB, 128)
         x_copy(t, 0).start()
         x_copy(t, 1).start()
@@ -276,39 +278,60 @@
         ahi[128 * slot + SL : 128 * slot + 128, :] = jnp.zeros((128 - SL, 1024), BF16)
         alo[128 * slot + SL : 128 * slot + 128, :] = jnp.zeros((128 - SL, 1024), BF16)
     wp_arrived(0)
+    split_w(0)
     far_step(0)
     for d in (1, 3, 0):
         split_s(d)
+    near_step(0)
+    w_arrived(1)
+    wp(1).start()
+    w_arrived(2)
+    wp(2).start()
+    wp_arrived(1)
+    split_w(1)
+    far_step(1)
 
     def step(t, _):
-        near_step(t)
+        join_step(t)
 
         @pl.when(t == 0)
         def _():
-            w_arrived(1)
-            wp(1).start()
-
-        @pl.when(t < 6)
-        def _():
-            w_arrived(t + 2)
-            wp(t + 2).start()
-
-        @pl.when(t == 2)
-        def _():
+            w_arrived(3)
+            wp(3).start()
+
+        @pl.when(t == 1)
+        def _():
+            w_arrived(4)
             q = chunk(y, 4)
+            wp(4).start()
             wy(4, q, 3, 5).start()
             wy(4, q, 1, 6).start()
             wy(4, q, 2, 7).start()
 
-        join_step(t)
+        @pl.when((t >= 2) & (t < 5))
+        def _():
+            w_arrived(t + 3)
+            wp(t + 3).start()
 
         @pl.when(t < 7)
         def _():
-            wp_arrived(t + 1)
-            far_step(t + 1)
+            near_step(t + 1)
+
+        @pl.when(t < 6)
+        def _():
+            wp_arrived(t + 2)
+            split_w(t + 2)
+            far_step(t + 2)
 
         @pl.when(t == 0)
         def _():
+            pl.semaphore_wait(tok_a, 3)
+            for d in (1, 2, 3):
+                pl.semaphore_signal(tok_b, inc=1, device_id=dev(x_=(x + d) % 4), device_id_type=MESH)
+
+        @pl.when(t == 1)
+        def _():
+            pl.semaphore_wait(tok_b, 3)
             c_swap().wait()
             ctp[c] = ctp[c] + cx[...]
             for d in range(4):
@@ -371,11 +394,6 @@
 
     lax.fori_loop(0, CH, step, 0)
     z_finish(5)
-    x_finish(7)
-    y_finish(3)
-    z_finish(6)
-    y_finish(4)
-
     c_pair().wait_send()
     c_pair_in().wait_recv()
 
@@ -388,7 +406,6 @@
         return 0
 
     lax.fori_loop(0, 8, split_c, 0)
-    y_finish(5)
 
     def project(t, d):
         yo = (y + 4 - d) % 4
@@ -401,7 +418,14 @@
         return 0
 
     pt[...] = jnp.zeros_like(pt)
-    lax.fori_loop(0, 24, project_some, 0)
+    lax.fori_loop(0, 4, project_some, 0)
+    x_finish(7)
+    z_finish(6)
+    y_finish(3)
+    y_finish(4)
+    lax.fori_loop(4, 20, project_some, 0)
+    y_finish(5)
+    lax.fori_loop(20, 24, project_some, 0)
     z_finish(7)
     y_finish(6)
     lax.fori_loop(24, 29, project_some, 0)
@@ -465,10 +489,6 @@
     m_copy(5).start()
     m_sum(x, 0)
     m_sum(x, 1)
-    for m in range(2, 6):
-        m_copy(m).wait_recv()
-    fs[...] = ms[x].reshape(8, 32, 128) + (mr[0] + mr[1]).reshape(8, 32, 128)
-
     def f_out(q):
         return rc(fs.at[q], frec.at[z], fsend.at[q], frecv.at[z], dev(y_=q // 2, zh_=q % 2, zl_=y))
 
@@ -476,11 +496,15 @@
         return rc(fs.at[0], frec.at[z_], fsend.at[0], frecv.at[z_], devz(z_, y_=zl))
 
     mine = y * 2 + zh
-    for q in range(8):
-
-        @pl.when(jnp.logical_not(diagonal & (q == mine)))
-        def _(q=q):
-            f_out(q).start()
+    for part in range(2):
+        m_copy(3 - part).wait_recv()
+        m_copy(4 + part).wait_recv()
+        fs[4 * part : 4 * part + 4] = ms[x, part] + (mr[0, part] + mr[1, part])
+        for q in range(4 * part, 4 * part + 4):
+
+            @pl.when(jnp.logical_not(diagonal & (q == mine)))
+            def _(q=q):
+                f_out(q).start()
 
     @pl.when(diagonal)
     def _():
@@ -554,6 +578,7 @@
         D((8,)), D((8,)), D((8,)), D((8,)), D((8,)),
         D((8, 6)), D((8, 6)), D((8, 3)), D((8, 3)), D((8, 3)), D((8, 3)),
         D((5,)), D((5,)), D((2, 5)), D((2, 5)), D((4,)), D((4,)), D((6,)), D((6,)), D((8,)), D((8,)),
+        pltpu.SemaphoreType.REGULAR, pltpu.SemaphoreType.REGULAR,
     ]
     return pl.pallas_call(
         kernel,

time: 106 us -> 102 us (0.962)
  Pallas kernels: 105 us -> 100 us
    pallas_call x1, Pallas kernels: 105 us -> 100 us  [on_device(): pl.pallas_call(kernel, out_shape=jax.ShapeDtypeStruct((64, 64), F32), in_...]
where the time goes in v4:
time: 102 us
  Pallas kernels  100 us (98%)
  local copies, waits for them, and re-layouts  1.38 us (1%)
    pallas_call x1, Pallas kernels, on_device(): pl.pallas_call(kernel, out_shape=jax.ShapeDtypeStruct((64, 64), F32), in_...  100 us

profile of v4, /device:TPU:1, one launch (start us, length us, event | category | flops | bytes accessed | tf_op | source)
XLA Modules:
  0.0 101.6 jit_solution(3013895106505331641)
XLA Ops:
  0.0 100.2 %shard_map.37 = f32[64,64]{1,0:T(8,128)} custom-call(f32[1536,512]{1,0:T(8,128)} %s_hbm.1, f32[64,512]{1,0:T(8,128)} %bitcast.1, f32[64,64]{1,0:T(8,128)} %c_hbm.1), custom_call_target="tpu_custom_call" | custom-call | tf_op jit(solution)/shard_map/pallas_call | solution.py:583
  100.3 1.4 %copy.5 = f32[64,64]{1,0:T(8,128)} copy(f32[64,64]{1,0:T(8,128)} %shard_map.37) | data formatting | bytes 32768

commit v5 on v4

--- a/solution.py
+++ b/solution.py
@@ -134,17 +134,6 @@
 
     split_s(2)
 
-    ccopy.wait()
-    ct_own = cv[...].T
-    cz = jnp.zeros((64, 64), F32)
-    at0 = jnp.concatenate([ct_own, cz], axis=1)
-    at1 = jnp.concatenate([cz, ct_own], axis=1)
-    ctp[...] = jnp.where(c == 0, at0, at1).reshape(2, 32, 128)
-
-    def c_swap():
-        return rc(ctp.at[1 - c], cx, csend.at[0], crecv.at[0], dev(c_=1 - c))
-
-    c_swap().start()
     qc = zl * 2 + zh
 
     def c_out(d):
@@ -274,22 +263,35 @@
             yo = (y + 4 - d) % 4
             keep(chunk(yo, t), yo)
 
-    for slot in range(NY):
-        ahi[128 * slot + SL : 128 * slot + 128, :] = jnp.zeros((128 - SL, 1024), BF16)
-        alo[128 * slot + SL : 128 * slot + 128, :] = jnp.zeros((128 - SL, 1024), BF16)
     wp_arrived(0)
     split_w(0)
     far_step(0)
-    for d in (1, 3, 0):
+    for d in (1, 3):
         split_s(d)
     near_step(0)
     w_arrived(1)
     wp(1).start()
-    w_arrived(2)
-    wp(2).start()
+    split_s(0)
+
+    ccopy.wait()
+    ct_own = cv[...].T
+    cz = jnp.zeros((64, 64), F32)
+    at0 = jnp.concatenate([ct_own, cz], axis=1)
+    at1 = jnp.concatenate([cz, ct_own], axis=1)
+    ctp[...] = jnp.where(c == 0, at0, at1).reshape(2, 32, 128)
+
+    def c_swap():
+        return rc(ctp.at[1 - c], cx, csend.at[0], crecv.at[0], dev(c_=1 - c))
+
+    c_swap().start()
+    for slot in range(NY):
+        ahi[128 * slot + SL : 128 * slot + 128, :] = jnp.zeros((128 - SL, 1024), BF16)
+        alo[128 * slot + SL : 128 * slot + 128, :] = jnp.zeros((128 - SL, 1024), BF16)
     wp_arrived(1)
     split_w(1)
     far_step(1)
+    w_arrived(2)
+    wp(2).start()
 
     def step(t, _):
         join_step(t)
@@ -382,18 +384,17 @@
         def _():
             x_finish(t - 1)
 
-        @pl.when(t >= 3)
-        def _():
-            z_finish(t - 3)
-
-        @pl.when(t >= 5)
-        def _():
-            y_finish(t - 5)
+        @pl.when(t >= 2)
+        def _():
+            z_finish(t - 2)
+
+        @pl.when(t >= 4)
+        def _():
+            y_finish(t - 4)
 
         return 0
 
     lax.fori_loop(0, CH, step, 0)
-    z_finish(5)
     c_pair().wait_send()
     c_pair_in().wait_recv()
 
@@ -421,7 +422,6 @@
     lax.fori_loop(0, 4, project_some, 0)
     x_finish(7)
     z_finish(6)
-    y_finish(3)
     y_finish(4)
     lax.fori_loop(4, 20, project_some, 0)
     y_finish(5)

time: 102 us -> 101 us (level)
  no operation moved by 1% of the time
where the time goes in v5:
time: 101 us
  Pallas kernels  99.5 us (99%)
  local copies, waits for them, and re-layouts  1.38 us (1%)
    pallas_call x1, Pallas kernels, on_device(): pl.pallas_call(kernel, out_shape=jax.ShapeDtypeStruct((64, 64), F32), in_...  99.5 us

profile of v5, /device:TPU:1, one launch (start us, length us, event | category | flops | bytes accessed | tf_op | source)
XLA Modules:
  0.0 100.8 jit_solution(2557442899442931165)
XLA Ops:
  0.0 99.5 %shard_map.37 = f32[64,64]{1,0:T(8,128)} custom-call(f32[1536,512]{1,0:T(8,128)} %s_hbm.1, f32[64,512]{1,0:T(8,128)} %bitcast.1, f32[64,64]{1,0:T(8,128)} %c_hbm.1), custom_call_target="tpu_custom_call" | custom-call | tf_op jit(solution)/shard_map/pallas_call | solution.py:583
  99.5 1.4 %copy.5 = f32[64,64]{1,0:T(8,128)} copy(f32[64,64]{1,0:T(8,128)} %shard_map.37) | data formatting | bytes 32768

commit v6 on v5

--- a/solution.py
+++ b/solution.py
@@ -70,6 +70,9 @@
         dy = u + (u // 2) * (1 - 2 * (u % 2))
         return ((y_ + dy) % 4) * 2 + (zh + t // 4) % 2
 
+    def lane(q):
+        return (q % 2) * 4 + q // 2
+
     q0 = chunk(y, 0)
     wcopy = pltpu.make_async_copy(w_hbm, wall.at[q0, c], lsem.at[0])
     ccopy = pltpu.make_async_copy(c_hbm, cv, lsem.at[1])
@@ -244,7 +247,7 @@
     def keep(q, yo):
         h, l = split(av[q, yo])
         rows = pl.ds(pl.multiple_of(yo * 128, 128), SL)
-        cols = pl.ds(pl.multiple_of(q * 128, 128), 128)
+        cols = pl.ds(pl.multiple_of(lane(q) * 128, 128), 128)
         ahi[rows, cols] = h
         alo[rows, cols] = l
 
@@ -399,7 +402,7 @@
     c_pair_in().wait_recv()
 
     def split_c(q, _):
-        cols = pl.ds(pl.multiple_of(q * 128, 128), 128)
+        cols = pl.ds(pl.multiple_of(lane(q) * 128, 128), 128)
         for half in range(2):
             h, l = split(ct[half, q].reshape(128, 128))
             chi[128 * half : 128 * half + 128, cols] = h
@@ -410,7 +413,7 @@
 
     def project(t, d):
         yo = (y + 4 - d) % 4
-        cols = pl.ds(pl.multiple_of(chunk(yo, t) * 128, 128), 128)
+        cols = pl.ds(pl.multiple_of(lane(chunk(yo, t)) * 128, 128), 128)
         slot = pl.ds(pl.multiple_of(yo * 128, 128), 128)
         pt[:, slot] = pt[:, slot] + three(nt, chi[:, cols], clo[:, cols], ahi[slot, cols], alo[slot, cols])
 
@@ -418,12 +421,18 @@
         project(n // 4, n % 4)
         return 0
 
-    pt[...] = jnp.zeros_like(pt)
-    lax.fori_loop(0, 4, project_some, 0)
     x_finish(7)
     z_finish(6)
     y_finish(4)
-    lax.fori_loop(4, 20, project_some, 0)
+
+    def project_side(n, _):
+        rows = pl.ds(pl.multiple_of(n * 128, 128), 128)
+        cols = pl.ds(pl.multiple_of(zh * 512, 512), 512)
+        pt[rows, :] = three(nt, chi[rows, cols], clo[rows, cols], ahi[:, cols], alo[:, cols])
+        return 0
+
+    lax.fori_loop(0, 2, project_side, 0)
+    lax.fori_loop(16, 20, project_some, 0)
     y_finish(5)
     lax.fori_loop(20, 24, project_some, 0)
     z_finish(7)
@@ -490,12 +499,12 @@
     m_sum(x, 0)
     m_sum(x, 1)
     def f_out(q):
-        return rc(fs.at[q], frec.at[z], fsend.at[q], frecv.at[z], dev(y_=q // 2, zh_=q % 2, zl_=y))
+        return rc(fs.at[q], frec.at[z], fsend.at[q], frecv.at[z], dev(y_=q % 4, zh_=q // 4, zl_=y))
 
     def f_in(z_):
         return rc(fs.at[0], frec.at[z_], fsend.at[0], frecv.at[z_], devz(z_, y_=zl))
 
-    mine = y * 2 + zh
+    mine = zh * 4 + y
     for part in range(2):
         m_copy(3 - part).wait_recv()
         m_copy(4 + part).wait_recv()

time: 101 us -> 100 us (0.990)
  no operation moved by 1% of the time
where the time goes in v6:
time: 100 us
  Pallas kernels  98.9 us (99%)
  local copies, waits for them, and re-layouts  1.38 us (1%)
    pallas_call x1, Pallas kernels, on_device(): pl.pallas_call(kernel, out_shape=jax.ShapeDtypeStruct((64, 64), F32), in_...  98.9 us

profile of v6, /device:TPU:1, one launch (start us, length us, event | category | flops | bytes accessed | tf_op | source)
XLA Modules:
  0.0 100.3 jit_solution(605540461423498909)
XLA Ops:
  0.0 98.9 %shard_map.37 = f32[64,64]{1,0:T(8,128)} custom-call(f32[1536,512]{1,0:T(8,128)} %s_hbm.1, f32[64,512]{1,0:T(8,128)} %bitcast.1, f32[64,64]{1,0:T(8,128)} %c_hbm.1), custom_call_target="tpu_custom_call" | custom-call | tf_op jit(solution)/shard_map/pallas_call | solution.py:592
  98.9 1.4 %copy.5 = f32[64,64]{1,0:T(8,128)} copy(f32[64,64]{1,0:T(8,128)} %shard_map.37) | data formatting | bytes 32768
